TPU v7x, 32 devices: a whole 2x2x4 slice. The times are simulated.
32 devices in a mesh: seq: 16 (over z, y, x), chan: 2 (over core).
Axes of the slice: x: 2, y: 2, z: 4, core: 2. Of those that a mesh axis runs over, the one named last changes fastest.
Arguments:
- values: bfloat16 [256, 8192], P('chan', 'seq'), may hold values from -6 to 6
- gate_one: bfloat16 [256, 8192], P('chan', 'seq'), may hold values from -6 to 6
- gate_two: bfloat16 [256, 8192], P('chan', 'seq'), may hold values from -6 to 6
- filter_one: float32 [256, 8192], P('chan', 'seq'), may hold values from -1 to 1
- filter_two: float32 [256, 8192], P('chan', 'seq'), may hold values from -1 to 1
- skip_one: float32 [256], P('chan'), may hold values from -1 to 1
- skip_two: float32 [256], P('chan'), may hold values from -1 to 1
- mix_weight: bfloat16 [256, 256], P(None, 'chan'), may hold values from -0.375 to 0.375
Outputs:
- mixed: bfloat16 [256, 8192], P('chan', 'seq')
All inputs are finite; a program needn't handle non-finite values.
Results may differ from a plain program's by a relative error of at most 0.0051.
Values may be sent and summed in bfloat16 or wider, within the bound.
A program may use at most 64 MiB of HBM per device.

v0:
```python
import math
import jax
import jax.numpy as jnp
from jax import lax
from jax.sharding import PartitionSpec as P

FOLD = 512
exact_mode = lax.Precision.HIGHEST


def angle_of(integers, modulus):
    return integers.astype(jnp.float32) * (2.0 * math.pi / modulus)


def fourier_rows(half_rows, column_count, period):
    row_index = lax.iota(jnp.int32, half_rows)[:, None]
    column_index = lax.iota(jnp.int32, column_count)[None, :]
    angles = angle_of(row_index * column_index % period, period)
    cosine = jnp.cos(angles)
    sine_tab = jnp.sin(angles)
    alternate = (1 - 2 * (row_index % 2)).astype(jnp.float32)
    sine_tab = jnp.where(column_index == 0, -alternate, sine_tab)
    return (cosine, sine_tab)


def fold_tables():
    points = lax.iota(jnp.int32, FOLD)
    angles = angle_of(points[:, None] * points[None, :] % FOLD, FOLD)
    return (jnp.cos(angles), jnp.sin(angles))


def spectra(columns_in):
    narrow = columns_in.shape[1]
    half_rows = columns_in.shape[2]
    period = 2 * half_rows
    modulus = period * FOLD
    seq_index = lax.axis_index("seq")
    cosine, sine_tab = fourier_rows(half_rows, half_rows, period)
    real_part = jnp.einsum("kra,ac->krc", columns_in, cosine, precision=exact_mode)
    imag_part = -jnp.einsum("kra,ac->krc", columns_in, sine_tab, precision=exact_mode)
    points_glob = seq_index * narrow + lax.iota(jnp.int32, narrow)
    column_index = lax.iota(jnp.int32, cosine.shape[1])
    angles = angle_of(points_glob[:, None] * column_index[None, :] % modulus, modulus)
    turn_cos = jnp.cos(angles)
    turn_sin = jnp.sin(angles)
    real_twist = real_part * turn_cos + imag_part * turn_sin
    imag_twist = imag_part * turn_cos - real_part * turn_sin
    real_recv, imag_recv = (
        lax.all_to_all(real_twist, "seq", split_axis=2, concat_axis=1, tiled=True),
        lax.all_to_all(imag_twist, "seq", split_axis=2, concat_axis=1, tiled=True),
    )
    row_count = real_recv.shape[2]
    is_leader = seq_index == 0
    spare_row = imag_recv
    phases = angle_of(lax.iota(jnp.int32, FOLD), 2 * FOLD)[None, :, None]
    row_mask = ((lax.iota(jnp.int32, row_count) == 0) & is_leader)[None, None, :]
    imag_recv = jnp.where(row_mask, 0.0, imag_recv)
    real_recv = jnp.concatenate([real_recv, spare_row * jnp.cos(phases)], axis=2)
    imag_recv = jnp.concatenate([imag_recv, -spare_row * jnp.sin(phases)], axis=2)
    rows_glob = jnp.concatenate(
        [
            seq_index * row_count + lax.iota(jnp.int32, row_count),
            jnp.full((1,), half_rows, jnp.int32),
        ]
    )
    cosine_q, sine_q = fold_tables()
    first_prod = jnp.einsum("kbr,bd->krd", real_recv + imag_recv, cosine_q, precision=exact_mode)
    second_prod = jnp.einsum("kbr,bd->krd", real_recv, -sine_q - cosine_q, precision=exact_mode)
    third_prod = jnp.einsum("kbr,bd->krd", imag_recv, cosine_q - sine_q, precision=exact_mode)
    return (first_prod - third_prod, first_prod + second_prod, rows_glob)


def inverse(spec_real, spectrum_imaginary, rows_glob, half_rows):
    period = 2 * half_rows
    modulus = period * FOLD
    seq_index = lax.axis_index("seq")
    cosine_q, sine_q = fold_tables()
    first_prod = jnp.einsum(
        "krd,db->kbr", spec_real + spectrum_imaginary, cosine_q, precision=exact_mode
    )
    second_prod = jnp.einsum("krd,db->kbr", spec_real, sine_q - cosine_q, precision=exact_mode)
    third_prod = jnp.einsum(
        "krd,db->kbr", spectrum_imaginary, cosine_q + sine_q, precision=exact_mode
    )
    real_part = first_prod - third_prod
    imag_part = first_prod + second_prod
    angles = angle_of(lax.iota(jnp.int32, FOLD)[:, None] * rows_glob[None, :] % modulus, modulus)
    turn_cos = jnp.cos(angles)
    turn_sin = jnp.sin(angles)
    real_twist = real_part * turn_cos - imag_part * turn_sin
    imag_twist = real_part * turn_sin + imag_part * turn_cos
    row_count = real_twist.shape[2] - 1
    row_mask = ((lax.iota(jnp.int32, row_count) == 0) & (seq_index == 0))[None, None, :]
    imag_send = jnp.where(row_mask, real_twist[:, :, row_count:], imag_twist[:, :, :row_count])
    real_recv, imag_recv = (
        lax.all_to_all(
            real_twist[:, :, :row_count], "seq", split_axis=1, concat_axis=2, tiled=True
        ),
        lax.all_to_all(imag_send, "seq", split_axis=1, concat_axis=2, tiled=True),
    )
    cosine, sine_tab = fourier_rows(half_rows, half_rows, period)
    coefficient_matrix = jnp.where(lax.iota(jnp.int32, half_rows) == 0, 1.0, 2.0).astype(
        jnp.float32
    )[None, :]
    cosine = cosine * coefficient_matrix
    sine_tab = sine_tab * coefficient_matrix
    result = jnp.einsum("kbc,ac->kba", real_recv, cosine, precision=exact_mode)
    result = result - jnp.einsum("kbc,ac->kba", imag_recv, sine_tab, precision=exact_mode)
    return result / modulus


def convolve(value_real, value_imag, filter_real, filter_imag, rows_glob, half_rows):
    prod_real = value_real * filter_real - value_imag * filter_imag
    prod_imag = value_real * filter_imag + value_imag * filter_real
    return inverse(prod_real, prod_imag, rows_glob, half_rows)


def per_device(values, gate_one, gate_two, filter_one, filter_two, skip_one, skip_two, mix_weight):
    channels, tokens = values.shape
    blocks = tokens // FOLD

    def columns(source):
        return jnp.swapaxes(source.reshape(channels, blocks, FOLD), 1, 2)

    def from_columns(result_cols):
        return jnp.swapaxes(result_cols, 1, 2).reshape(channels, tokens)

    def to_tokens(result_cols):
        return from_columns(
            lax.all_to_all(result_cols, "seq", split_axis=2, concat_axis=1, tiled=True)
        )

    values_cols = lax.all_to_all(columns(values), "seq", split_axis=1, concat_axis=2, tiled=True)
    filter_cols = (
        lax.all_to_all(columns(filter_one), "seq", split_axis=1, concat_axis=2, tiled=True),
        lax.all_to_all(columns(filter_two), "seq", split_axis=1, concat_axis=2, tiled=True),
    )
    values_wide = values_cols.astype(jnp.float32)
    half_rows = values_wide.shape[2]
    stacked = jnp.concatenate([values_wide, filter_cols[0], filter_cols[1]], axis=0)
    spec_real, spectrum_imaginary, rows_glob = spectra(stacked)
    conv_one = convolve(
        spec_real[:channels],
        spectrum_imaginary[:channels],
        spec_real[channels : 2 * channels],
        spectrum_imaginary[channels : 2 * channels],
        rows_glob,
        half_rows,
    )
    filter_two_real = spec_real[2 * channels :]
    filter_two_imag = spectrum_imaginary[2 * channels :]
    conv_tokens = to_tokens(conv_one)
    gated = gate_one.astype(jnp.float32) * (
        conv_tokens + skip_one[:, None] * values.astype(jnp.float32)
    )
    gated_cols = lax.all_to_all(columns(gated), "seq", split_axis=1, concat_axis=2, tiled=True)
    second_real, second_imag, restored_lines = spectra(gated_cols)
    conv_two = convolve(
        second_real, second_imag, filter_two_real, filter_two_imag, restored_lines, half_rows
    )
    second_tokens = to_tokens(conv_two)
    mixed_in = (gate_two.astype(jnp.float32) * (second_tokens + skip_two[:, None] * gated)).astype(
        jnp.bfloat16
    )
    summed = jnp.einsum(
        "de,dt->et",
        mix_weight,
        lax.all_gather(mixed_in, "chan", axis=0, tiled=True),
        preferred_element_type=jnp.float32,
    )
    return jax.nn.silu(summed).astype(jnp.bfloat16)


def solution(mesh):
    return jax.shard_map(
        per_device,
        mesh=mesh,
        in_specs=(
            P("chan", "seq"),
            P("chan", "seq"),
            P("chan", "seq"),
            P("chan", "seq"),
            P("chan", "seq"),
            P("chan"),
            P("chan"),
            P(None, "chan"),
        ),
        out_specs=P("chan", "seq"),
        check_vma=False,
    )
```

profile of v0, /device:TPU:0, one launch (start us, length us, event | category | flops | bytes accessed | tf_op | source)
XLA Modules:
  0.0 290.9 jit_solution(13032931578427769664)
XLA Ops:
  3.7 8.3 %all-to-all-start = ((bf16[16,2,2048]{2,1,0:T(2,128)(2,1)}), bf16[16,2,2048]{2,1,0:T(2,128)(2,1)S(1)}, u32[]{:S(2)}, u32[]{:S(2)}) async-start(bf16[16,2,2048]{2,1,0:T(2,128)(2,1)} %reshape.345), calls=%async_computation | async-start | bytes 262144 | tf_op jit(solution)/shard_map/all_to_all | solution.py:133
  13.9 6.0 %all-to-all-done = bf16[16,2,2048]{2,1,0:T(2,128)(2,1)S(1)} async-done(((bf16[16,2,2048]{2,1,0:T(2,128)(2,1)}), bf16[16,2,2048]{2,1,0:T(2,128)(2,1)S(1)}, u32[]{:S(2)}, u32[]{:S(2)}) %all-to-all-start) | async-done | bytes 131104 | tf_op jit(solution)/shard_map/all_to_all | solution.py:133
  24.3 7.6 %all-to-all-done.2 = f32[128,512,1]{0,2,1:T(1,128)S(1)} async-done(((f32[128,512,1]{0,2,1:T(1,128)}), f32[128,512,1]{0,2,1:T(1,128)S(1)}, u32[]{:S(2)}, u32[]{:S(2)}) %all-to-all-start.2) | async-done | bytes 262176 | tf_op jit(solution)/shard_map/all_to_all | solution.py:136
  36.2 8.4 %all-to-all-done.1 = f32[128,512,1]{0,2,1:T(1,128)S(1)} async-done(((f32[128,512,1]{0,2,1:T(1,128)}), f32[128,512,1]{0,2,1:T(1,128)S(1)}, u32[]{:S(2)}, u32[]{:S(2)}) %all-to-all-start.1) | async-done | bytes 262176 | tf_op jit(solution)/shard_map/all_to_all | solution.py:135
  52.6 17.7 %all-to-all-done.4 = f32[384,32,16]{0,1,2:T(8,128)S(1)} async-done(((f32[384,32,16]{0,1,2:T(8,128)}), f32[384,32,16]{0,1,2:T(8,128)S(1)}, u32[]{:S(2)}, u32[]{:S(2)}) %all-to-all-start.4) | async-done | bytes 786464 | tf_op jit(solution)/shard_map/all_to_all | solution.py:50
  76.1 17.9 %all-to-all-done.3 = f32[384,32,16]{0,1,2:T(8,128)S(1)} async-done(((f32[384,32,16]{0,1,2:T(8,128)}), f32[384,32,16]{0,1,2:T(8,128)S(1)}, u32[]{:S(2)}, u32[]{:S(2)}) %all-to-all-start.3) | async-done | bytes 786464 | tf_op jit(solution)/shard_map/all_to_all | solution.py:49
  94.5 6.5 %fusion = f32[384,2,512]{2,0,1:T(8,128)S(1)} fusion(f32[384,512,1]{1,0,2:T(8,128)S(1)} %get-tuple-element.16, f32[384,512,1]{1,0,2:T(8,128)S(1)} %get-tuple-element.17, f32[384,512,1]{1,0,2:T(8,128)S(1)} %get-tuple-element.15, f32[384,512,1]{1,0,2:T(8,128)S(1)} %copy.121), kind=kOutput, calls=%fused_computation.2 | convolution fusion | flops 2420768768 | bytes 4718592 | tf_op jit(solution)/shard_map/kbr,bd->krd/dot_general | solution.py:67
  101.0 7.1 %convolution_subtract_fusion = f32[384,2,512]{2,0,1:T(8,128)S(1)} fusion(f32[384,2,512]{2,0,1:T(8,128)S(1)} %fusion, f32[384,512,1]{1,0,2:T(8,128)S(1)} %get-tuple-element.16, f32[384,512,1]{1,0,2:T(8,128)S(1)} %get-tuple-element.17), kind=kOutput, calls=%fused_computation.8 | convolution fusion | flops 2420637696 | bytes 4718592 | tf_op jit(solution)/shard_map/kbr,bd->krd/dot_general | solution.py:69
  108.1 6.9 %convolution_add_fusion = f32[384,2,512]{2,0,1:T(8,128)S(1)} fusion(f32[384,2,512]{2,0,1:T(8,128)S(1)} %fusion, f32[384,512,1]{1,0,2:T(8,128)S(1)} %get-tuple-element.15, f32[384,512,1]{1,0,2:T(8,128)S(1)} %copy.121), kind=kOutput, calls=%fused_computation.7 | convolution fusion | flops 2420899840 | bytes 4718592 | tf_op jit(solution)/shard_map/kbr,bd->krd/dot_general | solution.py:68
  116.2 5.3 %fusion.20 = f32[512,128,2]{1,0,2:T(8,128)S(1)} fusion(f32[128,2,512]{2,0,1:T(8,128)S(1)} %get-tuple-element.8, f32[128,2,512]{2,0,1:T(8,128)S(1)} %get-tuple-element.7), kind=kOutput, calls=%fused_computation.38 | convolution fusion | flops 809107456 | bytes 1572864 | tf_op jit(solution)/shard_map/krd,db->kbr/dot_general | solution.py:78
  126.6 6.0 %add_bitcast_fusion.1 = (f32[128,512,2]{0,1,2:T(8,128)S(1)}, f32[128,512,2]{0,1,2:T(8,128)S(1)}) fusion(f32[512,128,2]{1,0,2:T(8,128)S(1)} %convolution_add_fusion.3, f32[512,2]{0,1:T(2,128)S(1)} %get-tuple-element.28, f32[512,2]{0,1:T(2,128)S(1)} %get-tuple-element.27, f32[512,128,2]{1,0,2:T(8,128)S(1)} %fusion.20, f32[128,2,512]{2,0,1:T(8,128)S(1)} %get-tuple-element.7), kind=kOutput, calls=%fused_computation.57 | convolution fusion | flops 810156032 | bytes 2629632 | tf_op jit(solution)/shard_map/krd,db->kbr/dot_general | solution.py:82
  133.4 13.2 %all_to_all.237 = f32[128,512,1]{0,2,1:T(1,128)S(1)} all-to-all(f32[128,512,1]{0,2,1:T(1,128)S(1)} %bitcast.205), channel_id=1, replica_groups=mesh['seq'=16,'chan'=2] {'seq'}, dimensions={1} | all-to-all | bytes 524288 | tf_op jit(solution)/shard_map/all_to_all | solution.py:96
  151.2 8.4 %all-to-all-done.6 = f32[128,512,1]{0,2,1:T(1,128)S(1)} async-done(((f32[128,512,1]{0,2,1:T(1,128)}), f32[128,512,1]{0,2,1:T(1,128)S(1)}, u32[]{:S(2)}, u32[]{:S(2)}) %all-to-all-start.6) | async-done | bytes 262176 | tf_op jit(solution)/shard_map/all_to_all | solution.py:99
  164.7 8.8 %all-to-all-done.7 = f32[128,32,16]{0,1,2:T(8,128)S(1)} async-done(((f32[128,32,16]{0,1,2:T(8,128)}), f32[128,32,16]{0,1,2:T(8,128)S(1)}, u32[]{:S(2)}, u32[]{:S(2)}) %all-to-all-start.7) | async-done | bytes 262176 | tf_op jit(solution)/shard_map/all_to_all | solution.py:130
  173.6 12.4 %all_to_all.238 = f32[128,512,1]{0,2,1:T(1,128)S(1)} all-to-all(f32[128,512,1]{0,2,1:T(1,128)S(1)} %bitcast.203), channel_id=1, replica_groups=mesh['seq'=16,'chan'=2] {'seq'}, dimensions={1} | all-to-all | bytes 524288 | tf_op jit(solution)/shard_map/all_to_all | solution.py:156
  192.4 8.3 %all-to-all-done.10 = f32[128,32,16]{0,1,2:T(8,128)S(1)} async-done(((f32[128,32,16]{0,1,2:T(8,128)}), f32[128,32,16]{0,1,2:T(8,128)S(1)}, u32[]{:S(2)}, u32[]{:S(2)}) %all-to-all-start.10) | async-done | bytes 262176 | tf_op jit(solution)/shard_map/all_to_all | solution.py:50
  204.4 8.9 %all-to-all-done.9 = f32[128,32,16]{0,1,2:T(8,128)S(1)} async-done(((f32[128,32,16]{0,1,2:T(8,128)}), f32[128,32,16]{0,1,2:T(8,128)S(1)}, u32[]{:S(2)}, u32[]{:S(2)}) %all-to-all-start.9) | async-done | bytes 262176 | tf_op jit(solution)/shard_map/all_to_all | solution.py:49
  213.3 5.6 %fusion.15 = f32[128,2,512]{2,0,1:T(8,128)S(1)} fusion(f32[128,512,1]{0,1,2:T(8,128)S(1)} %get-tuple-element.26, f32[128,512,1]{0,1,2:T(8,128)S(1)} %get-tuple-element.25, f32[128,512,1]{0,1,2:T(8,128)S(1)} %get-tuple-element.24, f32[128,512,1]{0,1,2:T(8,128)S(1)} %bitcast.217), kind=kOutput, calls=%fused_computation.33 | convolution fusion | flops 809369600 | bytes 1572864 | tf_op jit(solution)/shard_map/kbr,bd->krd/dot_general | solution.py:67
  218.9 6.3 %convolution_subtract_fusion.2 = f32[128,2,512]{2,0,1:T(8,128)S(1)} fusion(f32[128,2,512]{2,0,1:T(8,128)S(1)} %fusion.15, f32[128,512,1]{0,1,2:T(8,128)S(1)} %get-tuple-element.26, f32[128,512,1]{0,1,2:T(8,128)S(1)} %get-tuple-element.25), kind=kOutput, calls=%fused_computation.13 | convolution fusion | flops 809500672 | bytes 1572864 | tf_op jit(solution)/shard_map/kbr,bd->krd/dot_general | solution.py:69
  225.2 7.1 %multiply_add_fusion.1 = (f32[128,2,512]{2,0,1:T(8,128)S(1)}, f32[128,2,512]{2,0,1:T(8,128)S(1)}) fusion(f32[128,2,512]{2,0,1:T(8,128)S(1)} %convolution_subtract_fusion.2, f32[384,2,512]{2,0,1:T(8,128)} %copy-done.1, f32[384,2,512]{2,0,1:T(8,128)S(1)} %convolution_subtract_fusion, f32[128,2,512]{2,0,1:T(8,128)S(1)} %fusion.15, ...), kind=kOutput, calls=%fused_computation.54 | convolution fusion | flops 810549248 | bytes 3670016 | tf_op jit(solution)/shard_map/kbr,bd->krd/dot_general | solution.py:68
  237.2 5.3 %convolution_add_fusion.1 = f32[512,128,2]{1,0,2:T(8,128)S(1)} fusion(f32[512,128,2]{1,0,2:T(8,128)S(1)} %fusion.18, f32[128,2,512]{2,0,1:T(8,128)S(1)} %get-tuple-element.6), kind=kOutput, calls=%fused_computation.10 | convolution fusion | flops 809369600 | bytes 1572864 | tf_op jit(solution)/shard_map/krd,db->kbr/dot_general | solution.py:81
  248.5 12.4 %all_to_all.239 = f32[128,512,1]{0,2,1:T(1,128)S(1)} all-to-all(f32[128,512,1]{0,2,1:T(1,128)S(1)} %bitcast.204), channel_id=1, replica_groups=mesh['seq'=16,'chan'=2] {'seq'}, dimensions={1} | all-to-all | bytes 524288 | tf_op jit(solution)/shard_map/all_to_all | solution.py:96
  265.1 8.5 %all-to-all-done.12 = f32[128,512,1]{0,2,1:T(1,128)S(1)} async-done(((f32[128,512,1]{0,2,1:T(1,128)}), f32[128,512,1]{0,2,1:T(1,128)S(1)}, u32[]{:S(2)}, u32[]{:S(2)}) %all-to-all-start.12) | async-done | bytes 262176 | tf_op jit(solution)/shard_map/all_to_all | solution.py:99
  278.7 8.9 %all-to-all-done.13 = f32[128,32,16]{0,1,2:T(8,128)S(1)} async-done(((f32[128,32,16]{0,1,2:T(8,128)}), f32[128,32,16]{0,1,2:T(8,128)S(1)}, u32[]{:S(2)}, u32[]{:S(2)}) %all-to-all-start.13) | async-done | bytes 262176 | tf_op jit(solution)/shard_map/all_to_all | solution.py:130
  (77 shorter events, 78.1 us)
Async XLA Ops:
  0.0 289.7 %copy-start = (bf16[256,128]{1,0:T(8,128)(2,1)S(1)}, bf16[256,128]{1,0:T(8,128)(2,1)}, u32[]{:S(2)}) copy-start(bf16[256,128]{1,0:T(8,128)(2,1)} %param.15) | copy-start | bytes 196612
  0.0 23.4 %copy-start.3 = (f32[128,512]{1,0:T(8,128)S(1)}, f32[128,512]{1,0:T(8,128)}, u32[]{:S(2)}) copy-start(f32[128,512]{1,0:T(8,128)} %param.11) | copy-start | bytes 786436
  3.7 16.1 %all-to-all-start = ((bf16[16,2,2048]{2,1,0:T(2,128)(2,1)}), bf16[16,2,2048]{2,1,0:T(2,128)(2,1)S(1)}, u32[]{:S(2)}, u32[]{:S(2)}) async-start(bf16[16,2,2048]{2,1,0:T(2,128)(2,1)} %reshape.345), calls=%async_computation | async-start | bytes 262144 | tf_op jit(solution)/shard_map/all_to_all | solution.py:133
  19.9 12.0 %all-to-all-start.2 = ((f32[128,512,1]{0,2,1:T(1,128)}), f32[128,512,1]{0,2,1:T(1,128)S(1)}, u32[]{:S(2)}, u32[]{:S(2)}) async-start(f32[128,512,1]{0,2,1:T(1,128)} %bitcast.9), calls=%async_computation.2 | async-start | bytes 524288 | tf_op jit(solution)/shard_map/all_to_all | solution.py:136
  31.9 12.7 %all-to-all-start.1 = ((f32[128,512,1]{0,2,1:T(1,128)}), f32[128,512,1]{0,2,1:T(1,128)S(1)}, u32[]{:S(2)}, u32[]{:S(2)}) async-start(f32[128,512,1]{0,2,1:T(1,128)} %bitcast.5), calls=%async_computation.1 | async-start | bytes 524288 | tf_op jit(solution)/shard_map/all_to_all | solution.py:135
  47.9 22.5 %all-to-all-start.4 = ((f32[384,32,16]{0,1,2:T(8,128)}), f32[384,32,16]{0,1,2:T(8,128)S(1)}, u32[]{:S(2)}, u32[]{:S(2)}) async-start(f32[384,32,16]{0,1,2:T(8,128)} %copy.119), calls=%async_computation.4 | async-start | bytes 1572864 | tf_op jit(solution)/shard_map/all_to_all | solution.py:50
  70.4 23.6 %all-to-all-start.3 = ((f32[384,32,16]{0,1,2:T(8,128)}), f32[384,32,16]{0,1,2:T(8,128)S(1)}, u32[]{:S(2)}, u32[]{:S(2)}) async-start(f32[384,32,16]{0,1,2:T(8,128)} %copy.118), calls=%async_computation.3 | async-start | bytes 1572864 | tf_op jit(solution)/shard_map/all_to_all | solution.py:49
  115.0 1.2 copy-start.1
  146.7 17.8 %copy-start.2 = (bf16[128,512]{1,0:T(8,128)(2,1)S(1)}, bf16[128,512]{1,0:T(8,128)(2,1)}, u32[]{:S(2)}) copy-start(bf16[128,512]{1,0:T(8,128)(2,1)} %param.8) | copy-start | bytes 393220
  146.7 17.9 %copy-start.4 = (bf16[128,512]{1,0:T(8,128)(2,1)S(1)}, bf16[128,512]{1,0:T(8,128)(2,1)}, u32[]{:S(2)}) copy-start(bf16[128,512]{1,0:T(8,128)(2,1)} %param.9) | copy-start | bytes 393220
  146.7 12.9 %all-to-all-start.6 = ((f32[128,512,1]{0,2,1:T(1,128)}), f32[128,512,1]{0,2,1:T(1,128)S(1)}, u32[]{:S(2)}, u32[]{:S(2)}) async-start(f32[128,512,1]{0,2,1:T(1,128)} %bitcast.36), calls=%async_computation.6 | async-start | bytes 524288 | tf_op jit(solution)/shard_map/all_to_all | solution.py:99
  150.6 23.0 %copy-start.6 = (f32[128]{0:T(128)S(1)}, f32[128]{0:T(128)}, u32[]{:S(2)}) copy-start(f32[128]{0:T(128)} %param.13) | copy-start | bytes 1540
  160.9 12.7 %all-to-all-start.7 = ((f32[128,32,16]{0,1,2:T(8,128)}), f32[128,32,16]{0,1,2:T(8,128)S(1)}, u32[]{:S(2)}, u32[]{:S(2)}) async-start(f32[128,32,16]{0,1,2:T(8,128)} %copy.131), calls=%async_computation.7 | async-start | bytes 524288 | tf_op jit(solution)/shard_map/all_to_all | solution.py:130
  188.0 12.6 %all-to-all-start.10 = ((f32[128,32,16]{0,1,2:T(8,128)}), f32[128,32,16]{0,1,2:T(8,128)S(1)}, u32[]{:S(2)}, u32[]{:S(2)}) async-start(f32[128,32,16]{0,1,2:T(8,128)} %copy.138), calls=%async_computation.10 | async-start | bytes 524288 | tf_op jit(solution)/shard_map/all_to_all | solution.py:50
  200.7 12.6 %all-to-all-start.9 = ((f32[128,32,16]{0,1,2:T(8,128)}), f32[128,32,16]{0,1,2:T(8,128)S(1)}, u32[]{:S(2)}, u32[]{:S(2)}) async-start(f32[128,32,16]{0,1,2:T(8,128)} %copy.137), calls=%async_computation.9 | async-start | bytes 524288 | tf_op jit(solution)/shard_map/all_to_all | solution.py:49
  260.9 17.7 %copy-start.5 = (bf16[128,512]{1,0:T(8,128)(2,1)S(1)}, bf16[128,512]{1,0:T(8,128)(2,1)}, u32[]{:S(2)}) copy-start(bf16[128,512]{1,0:T(8,128)(2,1)} %param.10) | copy-start | bytes 393220
  260.9 26.7 %copy-start.7 = (f32[128]{0:T(128)S(1)}, f32[128]{0:T(128)}, u32[]{:S(2)}) copy-start(f32[128]{0:T(128)} %param.14) | copy-start | bytes 1540
  260.9 12.8 %all-to-all-start.12 = ((f32[128,512,1]{0,2,1:T(1,128)}), f32[128,512,1]{0,2,1:T(1,128)S(1)}, u32[]{:S(2)}, u32[]{:S(2)}) async-start(f32[128,512,1]{0,2,1:T(1,128)} %bitcast.69), calls=%async_computation.12 | async-start | bytes 524288 | tf_op jit(solution)/shard_map/all_to_all | solution.py:99
  275.0 12.6 %all-to-all-start.13 = ((f32[128,32,16]{0,1,2:T(8,128)}), f32[128,32,16]{0,1,2:T(8,128)S(1)}, u32[]{:S(2)}, u32[]{:S(2)}) async-start(f32[128,32,16]{0,1,2:T(8,128)} %copy.149), calls=%async_computation.13 | async-start | bytes 524288 | tf_op jit(solution)/shard_map/all_to_all | solution.py:130
where the time goes:
time: 297 us; the launch traced here: 291 us
  waiting for transfers between devices  110 us (37%)
  matrix products  76.8 us (26%)
  starting transfers between devices  46.1 us (16%)
  blocking collectives  40.1 us (14%)
  local copies, waits for them, and re-layouts  13.5 us (5%)
  other arithmetic  4.12 us (1%)
    all_to_all x2, waiting for transfers between devices, spectra(): lax.all_to_all(real_twist, 'seq', split_axis=2, concat_axis=1, tiled=True)  26.8 us
    all_to_all x2, waiting for transfers between devices, spectra(): lax.all_to_all(imag_twist, 'seq', split_axis=2, concat_axis=1, tiled=True)  26 us
    all_to_all x2, blocking collectives, inverse(): lax.all_to_all(real_twist[:, :, :row_count], 'seq', split_axis=1, concat_...  25.6 us
    all_to_all x2, waiting for transfers between devices, to_tokens(): lax.all_to_all(result_cols, 'seq', split_axis=2, concat_axis=1, tiled=True)  17.8 us
    all_to_all x2, waiting for transfers between devices, inverse(): lax.all_to_all(imag_send, 'seq', split_axis=1, concat_axis=2, tiled=True)  17 us
    dot_general x2, matrix products, spectra(): jnp.einsum('kbr,bd->krd', real_recv, -sine_q - cosine_q, precision=exact_...  14 us
    dot_general x2, matrix products, spectra(): jnp.einsum('kbr,bd->krd', imag_recv, cosine_q - sine_q, precision=exact_m...  13.4 us
    all_to_all x1, blocking collectives, per_device(): lax.all_to_all(columns(gated), 'seq', split_axis=1, concat_axis=2, tiled=...  12.4 us
  transfers between devices with their start and end apart: 11, of which 11 were waited for; matrix products, arithmetic and copies ran while one was open for 2% of the time, Pallas kernels for 0%

commit v1 on v0

--- a/solution.py
+++ b/solution.py
@@ -6,6 +6,13 @@
 
 FOLD = 512
 exact_mode = lax.Precision.HIGHEST
+
+
+def trade_parts(x, name, split, join):
+    size = lax.axis_size(name)
+    blocks = jnp.stack(jnp.split(x, size, axis=split), axis=0)
+    blocks = lax.all_to_all(blocks, name, split_axis=0, concat_axis=0)
+    return jnp.concatenate(blocks, axis=join)
 
 
 def angle_of(integers, modulus):
@@ -126,9 +133,7 @@
         return jnp.swapaxes(result_cols, 1, 2).reshape(channels, tokens)
 
     def to_tokens(result_cols):
-        return from_columns(
-            lax.all_to_all(result_cols, "seq", split_axis=2, concat_axis=1, tiled=True)
-        )
+        return from_columns(trade_parts(result_cols, "seq", 2, 1))
 
     values_cols = lax.all_to_all(columns(values), "seq", split_axis=1, concat_axis=2, tiled=True)
     filter_cols = (

time: 297 us -> 314 us (1.057)
  local copies, waits for them, and re-layouts: 13.5 us -> 31.6 us
    unnamed x24 -> x54, local copies, waits for them, and re-layouts: 5.27 us -> 23.3 us
where the time goes in v1:
time: 314 us; the launch traced here: 309 us
  waiting for transfers between devices  110 us (35%)
  matrix products  77 us (25%)
  starting transfers between devices  45.8 us (15%)
  blocking collectives  40.1 us (13%)
  local copies, waits for them, and re-layouts  31.6 us (10%)
  other arithmetic  4.1 us (1%)
    all_to_all x2, waiting for transfers between devices, spectra(): lax.all_to_all(real_twist, 'seq', split_axis=2, concat_axis=1, tiled=True)  26.8 us
    all_to_all x2, waiting for transfers between devices, spectra(): lax.all_to_all(imag_twist, 'seq', split_axis=2, concat_axis=1, tiled=True)  26 us
    all_to_all x2, blocking collectives, inverse(): lax.all_to_all(real_twist[:, :, :row_count], 'seq', split_axis=1, concat_...  25.6 us
    unnamed x54, local copies, waits for them, and re-layouts  23.3 us
    all_to_all x2, waiting for transfers between devices, trade_parts(): blocks = lax.all_to_all(blocks, name, split_axis=0, concat_axis=0)  17.8 us
    all_to_all x2, waiting for transfers between devices, inverse(): lax.all_to_all(imag_send, 'seq', split_axis=1, concat_axis=2, tiled=True)  16.9 us
    dot_general x2, matrix products, spectra(): jnp.einsum('kbr,bd->krd', real_recv, -sine_q - cosine_q, precision=exact_...  14 us
    dot_general x2, matrix products, spectra(): jnp.einsum('kbr,bd->krd', imag_recv, cosine_q - sine_q, precision=exact_m...  13.4 us
  transfers between devices with their start and end apart: 11, of which 11 were waited for; matrix products, arithmetic and copies ran while one was open for 2% of the time, Pallas kernels for 0%

profile of v1, /device:TPU:0, one launch (start us, length us, event | category | flops | bytes accessed | tf_op | source)
XLA Modules:
  0.0 308.9 jit_solution(7363179672169133475)
XLA Ops:
  3.7 8.3 %all-to-all-start = ((bf16[16,2,2048]{2,1,0:T(2,128)(2,1)}), bf16[16,2,2048]{2,1,0:T(2,128)(2,1)S(1)}, u32[]{:S(2)}, u32[]{:S(2)}) async-start(bf16[16,2,2048]{2,1,0:T(2,128)(2,1)} %reshape.351), calls=%async_computation | async-start | bytes 262144 | tf_op jit(solution)/shard_map/all_to_all | solution.py:138
  13.9 6.0 %all-to-all-done = bf16[16,2,2048]{2,1,0:T(2,128)(2,1)S(1)} async-done(((bf16[16,2,2048]{2,1,0:T(2,128)(2,1)}), bf16[16,2,2048]{2,1,0:T(2,128)(2,1)S(1)}, u32[]{:S(2)}, u32[]{:S(2)}) %all-to-all-start) | async-done | bytes 131104 | tf_op jit(solution)/shard_map/all_to_all | solution.py:138
  24.3 7.6 %all-to-all-done.2 = f32[128,512,1]{0,2,1:T(1,128)S(1)} async-done(((f32[128,512,1]{0,2,1:T(1,128)}), f32[128,512,1]{0,2,1:T(1,128)S(1)}, u32[]{:S(2)}, u32[]{:S(2)}) %all-to-all-start.2) | async-done | bytes 262176 | tf_op jit(solution)/shard_map/all_to_all | solution.py:141
  36.2 8.4 %all-to-all-done.1 = f32[128,512,1]{0,2,1:T(1,128)S(1)} async-done(((f32[128,512,1]{0,2,1:T(1,128)}), f32[128,512,1]{0,2,1:T(1,128)S(1)}, u32[]{:S(2)}, u32[]{:S(2)}) %all-to-all-start.1) | async-done | bytes 262176 | tf_op jit(solution)/shard_map/all_to_all | solution.py:140
  52.6 17.7 %all-to-all-done.4 = f32[384,32,16]{0,1,2:T(8,128)S(1)} async-done(((f32[384,32,16]{0,1,2:T(8,128)}), f32[384,32,16]{0,1,2:T(8,128)S(1)}, u32[]{:S(2)}, u32[]{:S(2)}) %all-to-all-start.4) | async-done | bytes 786464 | tf_op jit(solution)/shard_map/all_to_all | solution.py:57
  76.1 17.9 %all-to-all-done.3 = f32[384,32,16]{0,1,2:T(8,128)S(1)} async-done(((f32[384,32,16]{0,1,2:T(8,128)}), f32[384,32,16]{0,1,2:T(8,128)S(1)}, u32[]{:S(2)}, u32[]{:S(2)}) %all-to-all-start.3) | async-done | bytes 786464 | tf_op jit(solution)/shard_map/all_to_all | solution.py:56
  94.5 6.5 %fusion = f32[384,2,512]{2,0,1:T(8,128)S(1)} fusion(f32[384,512,1]{1,0,2:T(8,128)S(1)} %get-tuple-element.16, f32[384,512,1]{1,0,2:T(8,128)S(1)} %get-tuple-element.17, f32[384,512,1]{1,0,2:T(8,128)S(1)} %get-tuple-element.15, f32[384,512,1]{1,0,2:T(8,128)S(1)} %copy.208), kind=kOutput, calls=%fused_computation.2 | convolution fusion | flops 2420768768 | bytes 4718592 | tf_op jit(solution)/shard_map/kbr,bd->krd/dot_general | solution.py:74
  101.0 7.1 %convolution_subtract_fusion = f32[384,2,512]{2,0,1:T(8,128)S(1)} fusion(f32[384,2,512]{2,0,1:T(8,128)S(1)} %fusion, f32[384,512,1]{1,0,2:T(8,128)S(1)} %get-tuple-element.16, f32[384,512,1]{1,0,2:T(8,128)S(1)} %get-tuple-element.17), kind=kOutput, calls=%fused_computation.8 | convolution fusion | flops 2420637696 | bytes 4718592 | tf_op jit(solution)/shard_map/kbr,bd->krd/dot_general | solution.py:76
  108.1 6.9 %convolution_add_fusion = f32[384,2,512]{2,0,1:T(8,128)S(1)} fusion(f32[384,2,512]{2,0,1:T(8,128)S(1)} %fusion, f32[384,512,1]{1,0,2:T(8,128)S(1)} %get-tuple-element.15, f32[384,512,1]{1,0,2:T(8,128)S(1)} %copy.208), kind=kOutput, calls=%fused_computation.7 | convolution fusion | flops 2420899840 | bytes 4718592 | tf_op jit(solution)/shard_map/kbr,bd->krd/dot_general | solution.py:75
  116.2 5.3 %fusion.20 = f32[512,128,2]{1,0,2:T(8,128)S(1)} fusion(f32[128,2,512]{2,0,1:T(8,128)S(1)} %get-tuple-element.8, f32[128,2,512]{2,0,1:T(8,128)S(1)} %get-tuple-element.7), kind=kOutput, calls=%fused_computation.38 | convolution fusion | flops 809107456 | bytes 1572864 | tf_op jit(solution)/shard_map/krd,db->kbr/dot_general | solution.py:85
  126.6 6.2 %add_bitcast_fusion.1 = (f32[128,512,2]{0,1,2:T(8,128)S(1)}, f32[128,512,2]{0,1,2:T(8,128)S(1)}) fusion(f32[512,128,2]{1,0,2:T(8,128)S(1)} %convolution_add_fusion.3, f32[512,2]{0,1:T(2,128)S(1)} %get-tuple-element.60, f32[512,2]{0,1:T(2,128)S(1)} %get-tuple-element.59, f32[512,128,2]{1,0,2:T(8,128)S(1)} %fusion.20, f32[128,2,512]{2,0,1:T(8,128)S(1)} %get-tuple-element.7), kind=kOutput, calls=%fused_computation.57 | convolution fusion | flops 810156032 | bytes 2629632 | tf_op jit(solution)/shard_map/krd,db->kbr/dot_general | solution.py:89
  133.6 13.2 %all_to_all.217 = f32[128,512,1]{0,2,1:T(1,128)S(1)} all-to-all(f32[128,512,1]{0,2,1:T(1,128)S(1)} %bitcast.291), channel_id=1, replica_groups=mesh['seq'=16,'chan'=2] {'seq'}, dimensions={1} | all-to-all | bytes 524288 | tf_op jit(solution)/shard_map/all_to_all | solution.py:103
  151.2 8.4 %all-to-all-done.6 = f32[128,512,1]{0,2,1:T(1,128)S(1)} async-done(((f32[128,512,1]{0,2,1:T(1,128)}), f32[128,512,1]{0,2,1:T(1,128)S(1)}, u32[]{:S(2)}, u32[]{:S(2)}) %all-to-all-start.6) | async-done | bytes 262176 | tf_op jit(solution)/shard_map/all_to_all | solution.py:106
  173.8 8.8 %all-to-all-done.7 = f32[16,128,32,1]{1,2,3,0:T(8,128)S(1)} async-done(((f32[16,128,32,1]{1,2,3,0:T(8,128)}), f32[16,128,32,1]{1,2,3,0:T(8,128)S(1)}, u32[]{:S(2)}, u32[]{:S(2)}) %all-to-all-start.7) | async-done | bytes 262176 | tf_op jit(solution)/shard_map/all_to_all | solution.py:14
  182.7 12.4 %all_to_all.218 = f32[128,512,1]{0,2,1:T(1,128)S(1)} all-to-all(f32[128,512,1]{0,2,1:T(1,128)S(1)} %bitcast.289), channel_id=1, replica_groups=mesh['seq'=16,'chan'=2] {'seq'}, dimensions={1} | all-to-all | bytes 524288 | tf_op jit(solution)/shard_map/all_to_all | solution.py:161
  201.5 8.3 %all-to-all-done.10 = f32[128,32,16]{0,1,2:T(8,128)S(1)} async-done(((f32[128,32,16]{0,1,2:T(8,128)}), f32[128,32,16]{0,1,2:T(8,128)S(1)}, u32[]{:S(2)}, u32[]{:S(2)}) %all-to-all-start.10) | async-done | bytes 262176 | tf_op jit(solution)/shard_map/all_to_all | solution.py:57
  213.5 8.9 %all-to-all-done.9 = f32[128,32,16]{0,1,2:T(8,128)S(1)} async-done(((f32[128,32,16]{0,1,2:T(8,128)}), f32[128,32,16]{0,1,2:T(8,128)S(1)}, u32[]{:S(2)}, u32[]{:S(2)}) %all-to-all-start.9) | async-done | bytes 262176 | tf_op jit(solution)/shard_map/all_to_all | solution.py:56
  222.4 5.6 %fusion.15 = f32[128,2,512]{2,0,1:T(8,128)S(1)} fusion(f32[128,512,1]{0,1,2:T(8,128)S(1)} %get-tuple-element.42, f32[128,512,1]{0,1,2:T(8,128)S(1)} %get-tuple-element.41, f32[128,512,1]{0,1,2:T(8,128)S(1)} %get-tuple-element.40, f32[128,512,1]{0,1,2:T(8,128)S(1)} %bitcast.303), kind=kOutput, calls=%fused_computation.33 | convolution fusion | flops 809369600 | bytes 1572864 | tf_op jit(solution)/shard_map/kbr,bd->krd/dot_general | solution.py:74
  228.0 6.3 %convolution_subtract_fusion.2 = f32[128,2,512]{2,0,1:T(8,128)S(1)} fusion(f32[128,2,512]{2,0,1:T(8,128)S(1)} %fusion.15, f32[128,512,1]{0,1,2:T(8,128)S(1)} %get-tuple-element.42, f32[128,512,1]{0,1,2:T(8,128)S(1)} %get-tuple-element.41), kind=kOutput, calls=%fused_computation.13 | convolution fusion | flops 809500672 | bytes 1572864 | tf_op jit(solution)/shard_map/kbr,bd->krd/dot_general | solution.py:76
  234.3 7.1 %multiply_add_fusion.1 = (f32[128,2,512]{2,0,1:T(8,128)S(1)}, f32[128,2,512]{2,0,1:T(8,128)S(1)}) fusion(f32[128,2,512]{2,0,1:T(8,128)S(1)} %convolution_subtract_fusion.2, f32[384,2,512]{2,0,1:T(8,128)} %copy-done.1, f32[384,2,512]{2,0,1:T(8,128)S(1)} %convolution_subtract_fusion, f32[128,2,512]{2,0,1:T(8,128)S(1)} %fusion.15, ...), kind=kOutput, calls=%fused_computation.54 | convolution fusion | flops 810549248 | bytes 3670016 | tf_op jit(solution)/shard_map/kbr,bd->krd/dot_general | solution.py:75
  246.2 5.3 %convolution_add_fusion.1 = f32[512,128,2]{1,0,2:T(8,128)S(1)} fusion(f32[512,128,2]{1,0,2:T(8,128)S(1)} %fusion.18, f32[128,2,512]{2,0,1:T(8,128)S(1)} %get-tuple-element.6), kind=kOutput, calls=%fused_computation.10 | convolution fusion | flops 809369600 | bytes 1572864 | tf_op jit(solution)/shard_map/krd,db->kbr/dot_general | solution.py:88
  257.5 12.4 %all_to_all.219 = f32[128,512,1]{0,2,1:T(1,128)S(1)} all-to-all(f32[128,512,1]{0,2,1:T(1,128)S(1)} %bitcast.290), channel_id=1, replica_groups=mesh['seq'=16,'chan'=2] {'seq'}, dimensions={1} | all-to-all | bytes 524288 | tf_op jit(solution)/shard_map/all_to_all | solution.py:103
  274.1 8.5 %all-to-all-done.12 = f32[128,512,1]{0,2,1:T(1,128)S(1)} async-done(((f32[128,512,1]{0,2,1:T(1,128)}), f32[128,512,1]{0,2,1:T(1,128)S(1)}, u32[]{:S(2)}, u32[]{:S(2)}) %all-to-all-start.12) | async-done | bytes 262176 | tf_op jit(solution)/shard_map/all_to_all | solution.py:106
  296.6 8.9 %all-to-all-done.13 = f32[16,128,32,1]{1,2,3,0:T(8,128)S(1)} async-done(((f32[16,128,32,1]{1,2,3,0:T(8,128)}), f32[16,128,32,1]{1,2,3,0:T(8,128)S(1)}, u32[]{:S(2)}, u32[]{:S(2)}) %all-to-all-start.13) | async-done | bytes 262176 | tf_op jit(solution)/shard_map/all_to_all | solution.py:14
  (109 shorter events, 95.8 us)
Async XLA Ops:
  0.0 307.7 %copy-start = (bf16[256,128]{1,0:T(8,128)(2,1)S(1)}, bf16[256,128]{1,0:T(8,128)(2,1)}, u32[]{:S(2)}) copy-start(bf16[256,128]{1,0:T(8,128)(2,1)} %param.15) | copy-start | bytes 196612
  0.0 23.4 %copy-start.3 = (f32[128,512]{1,0:T(8,128)S(1)}, f32[128,512]{1,0:T(8,128)}, u32[]{:S(2)}) copy-start(f32[128,512]{1,0:T(8,128)} %param.11) | copy-start | bytes 786436
  3.7 16.1 %all-to-all-start = ((bf16[16,2,2048]{2,1,0:T(2,128)(2,1)}), bf16[16,2,2048]{2,1,0:T(2,128)(2,1)S(1)}, u32[]{:S(2)}, u32[]{:S(2)}) async-start(bf16[16,2,2048]{2,1,0:T(2,128)(2,1)} %reshape.351), calls=%async_computation | async-start | bytes 262144 | tf_op jit(solution)/shard_map/all_to_all | solution.py:138
  19.9 12.0 %all-to-all-start.2 = ((f32[128,512,1]{0,2,1:T(1,128)}), f32[128,512,1]{0,2,1:T(1,128)S(1)}, u32[]{:S(2)}, u32[]{:S(2)}) async-start(f32[128,512,1]{0,2,1:T(1,128)} %bitcast.9), calls=%async_computation.2 | async-start | bytes 524288 | tf_op jit(solution)/shard_map/all_to_all | solution.py:141
  31.9 12.7 %all-to-all-start.1 = ((f32[128,512,1]{0,2,1:T(1,128)}), f32[128,512,1]{0,2,1:T(1,128)S(1)}, u32[]{:S(2)}, u32[]{:S(2)}) async-start(f32[128,512,1]{0,2,1:T(1,128)} %bitcast.5), calls=%async_computation.1 | async-start | bytes 524288 | tf_op jit(solution)/shard_map/all_to_all | solution.py:140
  47.9 22.5 %all-to-all-start.4 = ((f32[384,32,16]{0,1,2:T(8,128)}), f32[384,32,16]{0,1,2:T(8,128)S(1)}, u32[]{:S(2)}, u32[]{:S(2)}) async-start(f32[384,32,16]{0,1,2:T(8,128)} %copy.206), calls=%async_computation.4 | async-start | bytes 1572864 | tf_op jit(solution)/shard_map/all_to_all | solution.py:57
  70.4 23.6 %all-to-all-start.3 = ((f32[384,32,16]{0,1,2:T(8,128)}), f32[384,32,16]{0,1,2:T(8,128)S(1)}, u32[]{:S(2)}, u32[]{:S(2)}) async-start(f32[384,32,16]{0,1,2:T(8,128)} %copy.205), calls=%async_computation.3 | async-start | bytes 1572864 | tf_op jit(solution)/shard_map/all_to_all | solution.py:56
  115.0 1.2 copy-start.1
  146.8 12.8 %all-to-all-start.6 = ((f32[128,512,1]{0,2,1:T(1,128)}), f32[128,512,1]{0,2,1:T(1,128)S(1)}, u32[]{:S(2)}, u32[]{:S(2)}) async-start(f32[128,512,1]{0,2,1:T(1,128)} %bitcast.36), calls=%async_computation.6 | async-start | bytes 524288 | tf_op jit(solution)/shard_map/all_to_all | solution.py:106
  150.6 22.9 %copy-start.2 = (bf16[128,512]{1,0:T(8,128)(2,1)S(1)}, bf16[128,512]{1,0:T(8,128)(2,1)}, u32[]{:S(2)}) copy-start(bf16[128,512]{1,0:T(8,128)(2,1)} %param.8) | copy-start | bytes 393220
  150.6 23.1 %copy-start.4 = (bf16[128,512]{1,0:T(8,128)(2,1)S(1)}, bf16[128,512]{1,0:T(8,128)(2,1)}, u32[]{:S(2)}) copy-start(bf16[128,512]{1,0:T(8,128)(2,1)} %param.9) | copy-start | bytes 393220
  151.2 31.5 %copy-start.6 = (f32[128]{0:T(128)S(1)}, f32[128]{0:T(128)}, u32[]{:S(2)}) copy-start(f32[128]{0:T(128)} %param.13) | copy-start | bytes 1540
  170.0 12.7 %all-to-all-start.7 = ((f32[16,128,32,1]{1,2,3,0:T(8,128)}), f32[16,128,32,1]{1,2,3,0:T(8,128)S(1)}, u32[]{:S(2)}, u32[]{:S(2)}) async-start(f32[16,128,32,1]{1,2,3,0:T(8,128)} %constant_dynamic-update-slice_fusion), calls=%async_computation.7 | async-start | bytes 524288 | tf_op jit(solution)/shard_map/all_to_all | solution.py:14
  197.1 12.6 %all-to-all-start.10 = ((f32[128,32,16]{0,1,2:T(8,128)}), f32[128,32,16]{0,1,2:T(8,128)S(1)}, u32[]{:S(2)}, u32[]{:S(2)}) async-start(f32[128,32,16]{0,1,2:T(8,128)} %copy.238), calls=%async_computation.10 | async-start | bytes 524288 | tf_op jit(solution)/shard_map/all_to_all | solution.py:57
  209.7 12.6 %all-to-all-start.9 = ((f32[128,32,16]{0,1,2:T(8,128)}), f32[128,32,16]{0,1,2:T(8,128)S(1)}, u32[]{:S(2)}, u32[]{:S(2)}) async-start(f32[128,32,16]{0,1,2:T(8,128)} %copy.237), calls=%async_computation.9 | async-start | bytes 524288 | tf_op jit(solution)/shard_map/all_to_all | solution.py:56
  269.9 12.6 %all-to-all-start.12 = ((f32[128,512,1]{0,2,1:T(1,128)}), f32[128,512,1]{0,2,1:T(1,128)S(1)}, u32[]{:S(2)}, u32[]{:S(2)}) async-start(f32[128,512,1]{0,2,1:T(1,128)} %bitcast.83), calls=%async_computation.12 | async-start | bytes 524288 | tf_op jit(solution)/shard_map/all_to_all | solution.py:106
  273.5 23.0 %copy-start.5 = (bf16[128,512]{1,0:T(8,128)(2,1)S(1)}, bf16[128,512]{1,0:T(8,128)(2,1)}, u32[]{:S(2)}) copy-start(bf16[128,512]{1,0:T(8,128)(2,1)} %param.10) | copy-start | bytes 393220
  273.5 32.1 %copy-start.7 = (f32[128]{0:T(128)S(1)}, f32[128]{0:T(128)}, u32[]{:S(2)}) copy-start(f32[128]{0:T(128)} %param.14) | copy-start | bytes 1540
  293.0 12.6 %all-to-all-start.13 = ((f32[16,128,32,1]{1,2,3,0:T(8,128)}), f32[16,128,32,1]{1,2,3,0:T(8,128)S(1)}, u32[]{:S(2)}, u32[]{:S(2)}) async-start(f32[16,128,32,1]{1,2,3,0:T(8,128)} %constant_dynamic-update-slice_fusion.16), calls=%async_computation.13 | async-start | bytes 524288 | tf_op jit(solution)/shard_map/all_to_all | solution.py:14
